TPU v7x, 32 devices: a whole 2x2x4 slice. The times are simulated.
32 devices in a mesh: layer: 8 (over z, x), panel: 4 (over y, core).
Axes of the slice: x: 2, y: 2, z: 4, core: 2. Of those that a mesh axis runs over, the one named last changes fastest.
Arguments:
- lower_blocks: bfloat16 [8, 512, 512], P('layer', 'panel'), may hold values from -2 to 0.5
- diag_blocks: bfloat16 [8, 512, 512], P('layer', 'panel'), may hold values from -0.5 to 4, as said below
- upper_blocks: bfloat16 [8, 512, 512], P('layer', 'panel'), may hold values from -2 to 0.5
- right_sides: bfloat16 [8, 512, 128], P('layer', 'panel'), may hold values from -6 to 6
Outputs:
- reduced_diag: bfloat16 [8, 512, 512], P('layer', 'panel')
- reduced_rhs: bfloat16 [8, 512, 128], P('layer', 'panel')
Inputs may be any that keep to these rules, and one draw needn't show every extreme that they name: `diag_blocks`: the diagonal entries of every diagonal block lie between 2 and 4.
All inputs are finite; a program needn't handle non-finite values.
Results may differ from a plain program's by a relative error of at most 0.035.
Values may be sent and summed in bfloat16 or wider, within the bound.
A program may use at most 64 MiB of HBM per device.

v0:
```python
import jax
import jax.numpy as jnp
from jax import lax
from jax.sharding import PartitionSpec as P

LEVELS = 3


def from_behind(shard, axis, by):
    size = lax.axis_size(axis)
    pairs = [(i, i + by) for i in range(size) if 0 <= i + by < size]
    return lax.ppermute(shard, axis, pairs)


def start_inverse(diag_block):
    inverse_diag = 1.0 / jnp.diagonal(diag_block).astype(jnp.float32)
    identity = jnp.eye(diag_block.shape[0], dtype=jnp.float32)
    guess = (
        2.0 * identity * inverse_diag[:, None]
        - inverse_diag[:, None] * diag_block.astype(jnp.float32) * inverse_diag[None, :]
    )
    return guess.astype(jnp.bfloat16)


def eliminate(diag_rows, rhs_rows, terms_left, terms_right, order_size):
    new_lower = (-terms_left[..., :order_size]).astype(jnp.bfloat16)
    new_diag = (
        diag_rows.astype(jnp.float32)
        - terms_left[..., order_size : 2 * order_size]
        - terms_right[..., :order_size]
    ).astype(jnp.bfloat16)
    new_upper = (-terms_right[..., order_size : 2 * order_size]).astype(jnp.bfloat16)
    new_rhs = (
        rhs_rows.astype(jnp.float32)
        - terms_left[..., 2 * order_size :]
        - terms_right[..., 2 * order_size :]
    ).astype(jnp.bfloat16)
    return (new_lower, new_diag, new_upper, new_rhs)


def on_device(lower_blocks, diag_blocks, upper_blocks, right_sides):
    lower_rows = lower_blocks[0]
    diag_rows = diag_blocks[0]
    upper_rows = upper_blocks[0]
    rhs_rows = right_sides[0]
    order_size = lower_rows.shape[1]
    for level_index in range(LEVELS):
        reach = 2**level_index
        full_diag, full_lower, full_upper, full_rhs = (
            lax.all_gather(diag_rows, "panel", axis=0, tiled=True),
            lax.all_gather(lower_rows, "panel", axis=0, tiled=True),
            lax.all_gather(upper_rows, "panel", axis=0, tiled=True),
            lax.all_gather(rhs_rows, "panel", axis=0, tiled=True),
        )
        stacked = jnp.concatenate([full_lower, full_upper, full_rhs], axis=1)
        guess_full = start_inverse(full_diag)
        product = jnp.dot(guess_full, full_diag, preferred_element_type=jnp.float32).astype(
            jnp.bfloat16
        )
        inverse = (
            2.0 * guess_full.astype(jnp.float32)
            - jnp.dot(product, guess_full, preferred_element_type=jnp.float32)
        ).astype(jnp.bfloat16)
        solved = jnp.dot(inverse, stacked, preferred_element_type=jnp.float32).astype(jnp.bfloat16)
        coupling_next = from_behind(lower_rows, "layer", -reach)
        coupling_prev = from_behind(upper_rows, "layer", reach)
        partial_next = jnp.dot(coupling_next, solved, preferred_element_type=jnp.float32)
        partial_prev = jnp.dot(coupling_prev, solved, preferred_element_type=jnp.float32)
        terms_left = from_behind(partial_next.astype(jnp.bfloat16), "layer", reach).astype(
            partial_next.dtype
        )
        terms_right = from_behind(partial_prev.astype(jnp.bfloat16), "layer", -reach).astype(
            partial_prev.dtype
        )
        lower_rows, diag_rows, upper_rows, rhs_rows = eliminate(
            diag_rows, rhs_rows, terms_left, terms_right, order_size
        )
    return (diag_rows[None], rhs_rows[None])


def solution(mesh):
    return jax.shard_map(
        on_device,
        mesh=mesh,
        in_specs=(
            P("layer", "panel", None),
            P("layer", "panel", None),
            P("layer", "panel", None),
            P("layer", "panel", None),
        ),
        out_specs=(P("layer", "panel", None), P("layer", "panel", None)),
        check_vma=False,
    )
```

profile of v0, /device:TPU:0, one launch (start us, length us, event | category | flops | bytes accessed | tf_op | source)
XLA Modules:
  0.0 187.6 jit_solution(5471749341740129736)
XLA Ops:
  0.6 0.0 copy-start.1
  0.6 0.0 copy-start
  0.6 5.0 %collective-permute-start.2 = (bf16[128,512]{1,0:T(8,128)(2,1)}, bf16[128,512]{1,0:T(8,128)(2,1)S(1)}, u32[]{:S(2)}, u32[]{:S(2)}) collective-permute-start(bf16[128,512]{1,0:T(8,128)(2,1)} %bitcast.57), channel_id=1, source_target_pairs={{0,4},{4,8},{8,12},{12,16},{16,20},{20,24},{24,28},{1,5},{5,9},{9,... | collective-permute-start | bytes 393224 | tf_op jit(solution)/shard_map/ppermute | solution.py:12
  5.7 1.3 collective-permute-start
  7.0 7.4 %all-gather.1 = bf16[1,512,512]{2,1,0:T(8,128)(2,1)S(1)} all-gather(bf16[1,128,512]{2,1,0:T(8,128)(2,1)} %param.4), channel_id=3, replica_groups=mesh['layer'=8,'panel'=4] {'panel'}, dimensions={1}, use_global_device_ids=true | all-gather | bytes 655360 | tf_op jit(solution)/shard_map/all_gather | solution.py:51
  14.4 7.5 %all-gather.2 = bf16[1,512,512]{2,1,0:T(8,128)(2,1)S(1)} all-gather(bf16[1,128,512]{2,1,0:T(8,128)(2,1)} %param.6), channel_id=4, replica_groups=mesh['layer'=8,'panel'=4] {'panel'}, dimensions={1}, use_global_device_ids=true | all-gather | bytes 655360 | tf_op jit(solution)/shard_map/all_gather | solution.py:52
  21.9 0.0 copy-done.1
  21.9 0.1 copy.15
  22.0 0.0 copy-done
  22.0 5.4 %all-gather.3 = bf16[1,512,128]{2,1,0:T(8,128)(2,1)S(1)} all-gather(bf16[1,128,128]{2,1,0:T(8,128)(2,1)S(1)} %copy-done), channel_id=5, replica_groups=mesh['layer'=8,'panel'=4] {'panel'}, dimensions={1}, use_global_device_ids=true | all-gather | bytes 163840 | tf_op jit(solution)/shard_map/all_gather | solution.py:53
  27.4 7.3 %all-gather = bf16[1,512,512]{1,2,0:T(8,128)(2,1)S(1)} all-gather(bf16[1,128,512]{1,2,0:T(8,128)(2,1)S(1)} %copy.15), channel_id=2, replica_groups=mesh['layer'=8,'panel'=4] {'panel'}, dimensions={1}, use_global_device_ids=true | all-gather | bytes 655360 | tf_op jit(solution)/shard_map/all_gather | solution.py:50
  34.7 4.8 %gather_fusion = bf16[512]{0:T(512)(128)(2,1)S(1)} fusion(bf16[512,512]{0,1:T(8,128)(2,1)S(1)} %bitcast.53, s32[512]{0:T(512)S(1)} %bitcast.50), kind=kCustom, calls=%fused_computation | custom fusion | bytes 6144 | tf_op jit(solution)/shard_map/jit(diagonal)/cond/branch_0_fun/gather | solution.py:16
  39.5 1.5 convolution_convert_fusion.11
  41.0 2.6 %convolution_convert_fusion.2 = bf16[512,1152]{1,0:T(8,128)(2,1)S(1)} fusion(bf16[512,512]{1,0:T(8,128)(2,1)} %convolution_convert_fusion.11, bf16[512,128]{1,0:T(8,128)(2,1)S(1)} %bitcast.58, bf16[512,512]{1,0:T(8,128)(2,1)S(1)} %bitcast.55, bf16[512,512]{1,0:T(8,128)(2,1)S(1)} %bitcast.54, f32[512]{0:T(512)S(1)} %convert_divide_fusion.2, ...), kind=kOutput, calls=%fused_computation.5 | convolution fusion | flops 881786880 | bytes 3409920 | tf_op jit(solution)/shard_map/dot_general | solution.py:64
  43.7 0.0 collective-permute-done
  43.7 0.5 fusion
  44.2 4.6 %collective-permute-start.1 = (bf16[128,1152]{0,1:T(8,128)(2,1)S(1)}, bf16[128,1152]{0,1:T(8,128)(2,1)S(1)}, u32[]{:S(2)}, u32[]{:S(2)}) collective-permute-start(bf16[128,1152]{0,1:T(8,128)(2,1)S(1)} %fusion), channel_id=1, source_target_pairs={{0,4},{4,8},{8,12},{12,16},{16,20},{20,24},{24,28},{1,5},{5,9},{9,... | collective-permute-start | bytes 884744 | tf_op jit(solution)/shard_map/ppermute | solution.py:12
  48.8 0.0 collective-permute-done.2
  48.8 0.5 fusion.1
  49.3 1.3 collective-permute-start.3
  50.6 0.1 copy.17
  50.7 11.1 %collective-permute-done.1 = bf16[128,1152]{0,1:T(8,128)(2,1)S(1)} collective-permute-done((bf16[128,1152]{0,1:T(8,128)(2,1)S(1)}, bf16[128,1152]{0,1:T(8,128)(2,1)S(1)}, u32[]{:S(2)}, u32[]{:S(2)}) %collective-permute-start.1) | collective-permute-done | bytes 294944 | tf_op jit(solution)/shard_map/ppermute | solution.py:12
  61.9 0.0 collective-permute-done.3
  61.9 0.1 fusion.40
  62.0 1.3 collective-permute-start.4
  63.3 6.6 %all_gather.41 = bf16[512,512]{0,1:T(8,128)(2,1)S(1)} all-gather(bf16[128,512]{0,1:T(8,128)(2,1)S(1)} %get-tuple-element.9), channel_id=1, replica_groups=mesh['layer'=8,'panel'=4] {'panel'}, dimensions={0}, use_global_device_ids=true | all-gather | bytes 655360 | tf_op jit(solution)/shard_map/all_gather | solution.py:51
  69.9 7.3 %collective-permute-start.6 = (bf16[128,512]{0,1:T(8,128)(2,1)S(1)}, bf16[128,512]{0,1:T(8,128)(2,1)S(1)}, u32[]{:S(2)}, u32[]{:S(2)}) collective-permute-start(bf16[128,512]{0,1:T(8,128)(2,1)S(1)} %get-tuple-element.11), channel_id=1, source_target_pairs={{0,8},{4,12},{8,16},{12,20},{16,24},{20,28},{1,9},{5,13},{9,17},{1... | collective-permute-start | bytes 393224 | tf_op jit(solution)/shard_map/ppermute | solution.py:12
  77.2 7.0 %all_gather.42 = bf16[512,512]{0,1:T(8,128)(2,1)S(1)} all-gather(bf16[128,512]{0,1:T(8,128)(2,1)S(1)} %get-tuple-element.11), channel_id=1, replica_groups=mesh['layer'=8,'panel'=4] {'panel'}, dimensions={0}, use_global_device_ids=true | all-gather | bytes 655360 | tf_op jit(solution)/shard_map/all_gather | solution.py:52
  84.2 5.9 %all_gather.43 = bf16[512,128]{0,1:T(8,128)(2,1)} all-gather(bf16[128,128]{0,1:T(8,128)(2,1)S(1)} %fusion.54), channel_id=1, replica_groups=mesh['layer'=8,'panel'=4] {'panel'}, dimensions={0}, use_global_device_ids=true | all-gather | bytes 163840 | tf_op jit(solution)/shard_map/all_gather | solution.py:53
  90.1 7.3 %all_gather.40 = bf16[512,512]{0,1:T(8,128)(2,1)S(1)} all-gather(bf16[128,512]{0,1:T(8,128)(2,1)S(1)} %get-tuple-element.10), channel_id=1, replica_groups=mesh['layer'=8,'panel'=4] {'panel'}, dimensions={0}, use_global_device_ids=true | all-gather | bytes 655360 | tf_op jit(solution)/shard_map/all_gather | solution.py:50
  97.4 4.8 %gather_fusion.1 = bf16[512]{0:T(512)(128)(2,1)S(1)} fusion(bf16[512,512]{0,1:T(8,128)(2,1)S(1)} %all_gather.40, s32[512]{0:T(512)S(1)} %bitcast.51), kind=kCustom, calls=%fused_computation.1 | custom fusion | bytes 6144 | tf_op jit(solution)/shard_map/jit(diagonal)/cond/branch_0_fun/gather | solution.py:16
  102.2 1.5 convolution_convert_fusion.10
  103.7 2.6 %convolution_convert_fusion.1 = bf16[512,1152]{1,0:T(8,128)(2,1)S(1)} fusion(bf16[512,512]{1,0:T(8,128)(2,1)} %convolution_convert_fusion.10, bf16[512,128]{0,1:T(8,128)(2,1)} %all_gather.43, bf16[512,512]{0,1:T(8,128)(2,1)S(1)} %all_gather.42, bf16[512,512]{0,1:T(8,128)(2,1)S(1)} %all_gather.41, bf16[512,512]{0,1:T(8,128)(2,1)S(1)} %all_gather.40, ...), kind=kOutput, calls=%fused_computation.4 | convolution fusion | flops 881786880 | bytes 3409920 | tf_op jit(solution)/shard_map/dot_general | solution.py:64
  106.3 0.0 collective-permute-done.4
  106.4 0.6 convolution_convert_fusion.6
  107.0 3.7 %collective-permute-start.5 = (bf16[128,1152]{0,1:T(8,128)(2,1)S(1)}, bf16[128,1152]{0,1:T(8,128)(2,1)S(1)}, u32[]{:S(2)}, u32[]{:S(2)}) collective-permute-start(bf16[128,1152]{0,1:T(8,128)(2,1)S(1)} %convolution_convert_fusion.6), channel_id=1, source_target_pairs={{0,8},{4,12},{8,16},{12,20},{16,24},{20,28},{1,9},{5,13},{9,17},{1... | collective-permute-start | bytes 884744 | tf_op jit(solution)/shard_map/ppermute | solution.py:12
  110.6 0.0 collective-permute-done.6
  110.7 0.6 convolution_convert_fusion.5
  111.3 1.3 collective-permute-start.7
  112.6 4.8 %collective-permute-done.5 = bf16[128,1152]{0,1:T(8,128)(2,1)S(1)} collective-permute-done((bf16[128,1152]{0,1:T(8,128)(2,1)S(1)}, bf16[128,1152]{0,1:T(8,128)(2,1)S(1)}, u32[]{:S(2)}, u32[]{:S(2)}) %collective-permute-start.5) | collective-permute-done | bytes 294944 | tf_op jit(solution)/shard_map/ppermute | solution.py:12
  117.4 4.7 %collective-permute-done.7 = bf16[128,1152]{0,1:T(8,128)(2,1)S(1)} collective-permute-done((bf16[128,1152]{0,1:T(8,128)(2,1)S(1)}, bf16[128,1152]{0,1:T(8,128)(2,1)S(1)}, u32[]{:S(2)}, u32[]{:S(2)}) %collective-permute-start.7) | collective-permute-done | bytes 294944 | tf_op jit(solution)/shard_map/ppermute | solution.py:12
  122.2 0.1 fusion.37
  122.3 1.3 collective-permute-start.8
  123.6 6.7 %all_gather.45 = bf16[512,512]{0,1:T(8,128)(2,1)S(1)} all-gather(bf16[128,512]{0,1:T(8,128)(2,1)S(1)} %get-tuple-element.6), channel_id=1, replica_groups=mesh['layer'=8,'panel'=4] {'panel'}, dimensions={0}, use_global_device_ids=true | all-gather | bytes 655360 | tf_op jit(solution)/shard_map/all_gather | solution.py:51
  130.3 5.4 %collective-permute-start.10 = (bf16[128,512]{0,1:T(8,128)(2,1)S(1)}, bf16[128,512]{0,1:T(8,128)(2,1)S(1)}, u32[]{:S(2)}, u32[]{:S(2)}) collective-permute-start(bf16[128,512]{0,1:T(8,128)(2,1)S(1)} %get-tuple-element.8), channel_id=1, source_target_pairs={{0,16},{4,20},{8,24},{12,28},{1,17},{5,21},{9,25},{13,29},{2,18},{... | collective-permute-start | bytes 393224 | tf_op jit(solution)/shard_map/ppermute | solution.py:12
  135.8 7.0 %all_gather.46 = bf16[512,512]{0,1:T(8,128)(2,1)S(1)} all-gather(bf16[128,512]{0,1:T(8,128)(2,1)S(1)} %get-tuple-element.8), channel_id=1, replica_groups=mesh['layer'=8,'panel'=4] {'panel'}, dimensions={0}, use_global_device_ids=true | all-gather | bytes 655360 | tf_op jit(solution)/shard_map/all_gather | solution.py:52
  142.8 5.9 %all_gather.47 = bf16[512,128]{0,1:T(8,128)(2,1)} all-gather(bf16[128,128]{0,1:T(8,128)(2,1)S(1)} %fusion.53), channel_id=1, replica_groups=mesh['layer'=8,'panel'=4] {'panel'}, dimensions={0}, use_global_device_ids=true | all-gather | bytes 163840 | tf_op jit(solution)/shard_map/all_gather | solution.py:53
  148.7 7.5 %all_gather.44 = bf16[512,512]{0,1:T(8,128)(2,1)S(1)} all-gather(bf16[128,512]{0,1:T(8,128)(2,1)S(1)} %get-tuple-element.7), channel_id=1, replica_groups=mesh['layer'=8,'panel'=4] {'panel'}, dimensions={0}, use_global_device_ids=true | all-gather | bytes 655360 | tf_op jit(solution)/shard_map/all_gather | solution.py:50
  156.1 4.8 %gather_fusion.2 = bf16[512]{0:T(512)(128)(2,1)S(1)} fusion(bf16[512,512]{0,1:T(8,128)(2,1)S(1)} %all_gather.44, s32[512]{0:T(512)S(1)} %bitcast.52), kind=kCustom, calls=%fused_computation.2 | custom fusion | bytes 6144 | tf_op jit(solution)/shard_map/jit(diagonal)/cond/branch_0_fun/gather | solution.py:16
  160.9 1.5 convolution_convert_fusion.9
  162.4 2.6 %convolution_convert_fusion = bf16[512,1152]{1,0:T(8,128)(2,1)S(1)} fusion(bf16[512,512]{1,0:T(8,128)(2,1)} %convolution_convert_fusion.9, bf16[512,128]{0,1:T(8,128)(2,1)} %all_gather.47, bf16[512,512]{0,1:T(8,128)(2,1)S(1)} %all_gather.46, bf16[512,512]{0,1:T(8,128)(2,1)S(1)} %all_gather.45, bf16[512,512]{0,1:T(8,128)(2,1)S(1)} %all_gather.44, ...), kind=kOutput, calls=%fused_computation.3 | convolution fusion | flops 881786880 | bytes 3409920 | tf_op jit(solution)/shard_map/dot_general | solution.py:64
  165.1 0.0 collective-permute-done.8
  165.1 0.6 convolution_convert_fusion.4
  165.7 1.6 collective-permute-start.9
  167.3 0.0 collective-permute-done.10
  167.3 0.6 convolution_convert_fusion.3
  167.9 1.3 collective-permute-start.11
  169.2 4.9 %collective-permute-done.9 = bf16[128,1152]{0,1:T(8,128)(2,1)S(1)} collective-permute-done((bf16[128,1152]{0,1:T(8,128)(2,1)S(1)}, bf16[128,1152]{0,1:T(8,128)(2,1)S(1)}, u32[]{:S(2)}, u32[]{:S(2)}) %collective-permute-start.9) | collective-permute-done | bytes 294944 | tf_op jit(solution)/shard_map/ppermute | solution.py:12
  174.1 11.9 %collective-permute-done.11 = bf16[128,1152]{0,1:T(8,128)(2,1)S(1)} collective-permute-done((bf16[128,1152]{0,1:T(8,128)(2,1)S(1)}, bf16[128,1152]{0,1:T(8,128)(2,1)S(1)}, u32[]{:S(2)}, u32[]{:S(2)}) %collective-permute-start.11) | collective-permute-done | bytes 294944 | tf_op jit(solution)/shard_map/ppermute | solution.py:12
  186.1 0.8 copy.22
  186.9 0.7 copy.23
  (14 shorter events, 0.4 us)
Async XLA Ops:
  0.6 21.2 %copy-start.1 = (bf16[1,128,512]{2,1,0:T(8,128)(2,1)S(1)}, bf16[1,128,512]{2,1,0:T(8,128)(2,1)}, u32[]{:S(2)}) copy-start(bf16[1,128,512]{2,1,0:T(8,128)(2,1)} %param.5) | copy-start | bytes 393220
  0.6 21.4 %copy-start = (bf16[1,128,128]{2,1,0:T(8,128)(2,1)S(1)}, bf16[1,128,128]{2,1,0:T(8,128)(2,1)}, u32[]{:S(2)}) copy-start(bf16[1,128,128]{2,1,0:T(8,128)(2,1)} %param.7) | copy-start | bytes 98308
  0.6 48.1 %collective-permute-start.2 = (bf16[128,512]{1,0:T(8,128)(2,1)}, bf16[128,512]{1,0:T(8,128)(2,1)S(1)}, u32[]{:S(2)}, u32[]{:S(2)}) collective-permute-start(bf16[128,512]{1,0:T(8,128)(2,1)} %bitcast.57), channel_id=1, source_target_pairs={{0,4},{4,8},{8,12},{12,16},{16,20},{20,24},{24,28},{1,5},{5,9},{9,... | collective-permute-start | bytes 393224 | tf_op jit(solution)/shard_map/ppermute | solution.py:12
  5.7 38.0 %collective-permute-start = (bf16[128,512]{1,0:T(8,128)(2,1)}, bf16[128,512]{1,0:T(8,128)(2,1)S(1)}, u32[]{:S(2)}, u32[]{:S(2)}) collective-permute-start(bf16[128,512]{1,0:T(8,128)(2,1)} %bitcast.56), channel_id=1, source_target_pairs={{4,0},{8,4},{12,8},{16,12},{20,16},{24,20},{28,24},{5,1},{9,5},{13... | collective-permute-start | bytes 393224 | tf_op jit(solution)/shard_map/ppermute | solution.py:12
  44.2 17.6 %collective-permute-start.1 = (bf16[128,1152]{0,1:T(8,128)(2,1)S(1)}, bf16[128,1152]{0,1:T(8,128)(2,1)S(1)}, u32[]{:S(2)}, u32[]{:S(2)}) collective-permute-start(bf16[128,1152]{0,1:T(8,128)(2,1)S(1)} %fusion), channel_id=1, source_target_pairs={{0,4},{4,8},{8,12},{12,16},{16,20},{20,24},{24,28},{1,5},{5,9},{9,... | collective-permute-start | bytes 884744 | tf_op jit(solution)/shard_map/ppermute | solution.py:12
  49.3 12.6 %collective-permute-start.3 = (bf16[128,1152]{0,1:T(8,128)(2,1)S(1)}, bf16[128,1152]{0,1:T(8,128)(2,1)S(1)}, u32[]{:S(2)}, u32[]{:S(2)}) collective-permute-start(bf16[128,1152]{0,1:T(8,128)(2,1)S(1)} %fusion.1), channel_id=1, source_target_pairs={{4,0},{8,4},{12,8},{16,12},{20,16},{24,20},{28,24},{5,1},{9,5},{13... | collective-permute-start | bytes 884744 | tf_op jit(solution)/shard_map/ppermute | solution.py:12
  62.0 44.3 %collective-permute-start.4 = (bf16[128,512]{0,1:T(8,128)(2,1)S(1)}, bf16[128,512]{0,1:T(8,128)(2,1)S(1)}, u32[]{:S(2)}, u32[]{:S(2)}) collective-permute-start(bf16[128,512]{0,1:T(8,128)(2,1)S(1)} %get-tuple-element.9), channel_id=1, source_target_pairs={{8,0},{12,4},{16,8},{20,12},{24,16},{28,20},{9,1},{13,5},{17,9},{2... | collective-permute-start | bytes 393224 | tf_op jit(solution)/shard_map/ppermute | solution.py:12
  69.9 40.8 %collective-permute-start.6 = (bf16[128,512]{0,1:T(8,128)(2,1)S(1)}, bf16[128,512]{0,1:T(8,128)(2,1)S(1)}, u32[]{:S(2)}, u32[]{:S(2)}) collective-permute-start(bf16[128,512]{0,1:T(8,128)(2,1)S(1)} %get-tuple-element.11), channel_id=1, source_target_pairs={{0,8},{4,12},{8,16},{12,20},{16,24},{20,28},{1,9},{5,13},{9,17},{1... | collective-permute-start | bytes 393224 | tf_op jit(solution)/shard_map/ppermute | solution.py:12
  107.0 10.4 %collective-permute-start.5 = (bf16[128,1152]{0,1:T(8,128)(2,1)S(1)}, bf16[128,1152]{0,1:T(8,128)(2,1)S(1)}, u32[]{:S(2)}, u32[]{:S(2)}) collective-permute-start(bf16[128,1152]{0,1:T(8,128)(2,1)S(1)} %convolution_convert_fusion.6), channel_id=1, source_target_pairs={{0,8},{4,12},{8,16},{12,20},{16,24},{20,28},{1,9},{5,13},{9,17},{1... | collective-permute-start | bytes 884744 | tf_op jit(solution)/shard_map/ppermute | solution.py:12
  111.3 10.9 %collective-permute-start.7 = (bf16[128,1152]{0,1:T(8,128)(2,1)S(1)}, bf16[128,1152]{0,1:T(8,128)(2,1)S(1)}, u32[]{:S(2)}, u32[]{:S(2)}) collective-permute-start(bf16[128,1152]{0,1:T(8,128)(2,1)S(1)} %convolution_convert_fusion.5), channel_id=1, source_target_pairs={{8,0},{12,4},{16,8},{20,12},{24,16},{28,20},{9,1},{13,5},{17,9},{2... | collective-permute-start | bytes 884744 | tf_op jit(solution)/shard_map/ppermute | solution.py:12
  122.3 42.8 %collective-permute-start.8 = (bf16[128,512]{0,1:T(8,128)(2,1)S(1)}, bf16[128,512]{0,1:T(8,128)(2,1)S(1)}, u32[]{:S(2)}, u32[]{:S(2)}) collective-permute-start(bf16[128,512]{0,1:T(8,128)(2,1)S(1)} %get-tuple-element.6), channel_id=1, source_target_pairs={{16,0},{20,4},{24,8},{28,12},{17,1},{21,5},{25,9},{29,13},{18,2},{... | collective-permute-start | bytes 393224 | tf_op jit(solution)/shard_map/ppermute | solution.py:12
  130.3 37.0 %collective-permute-start.10 = (bf16[128,512]{0,1:T(8,128)(2,1)S(1)}, bf16[128,512]{0,1:T(8,128)(2,1)S(1)}, u32[]{:S(2)}, u32[]{:S(2)}) collective-permute-start(bf16[128,512]{0,1:T(8,128)(2,1)S(1)} %get-tuple-element.8), channel_id=1, source_target_pairs={{0,16},{4,20},{8,24},{12,28},{1,17},{5,21},{9,25},{13,29},{2,18},{... | collective-permute-start | bytes 393224 | tf_op jit(solution)/shard_map/ppermute | solution.py:12
  165.7 8.4 %collective-permute-start.9 = (bf16[128,1152]{0,1:T(8,128)(2,1)S(1)}, bf16[128,1152]{0,1:T(8,128)(2,1)S(1)}, u32[]{:S(2)}, u32[]{:S(2)}) collective-permute-start(bf16[128,1152]{0,1:T(8,128)(2,1)S(1)} %convolution_convert_fusion.4), channel_id=1, source_target_pairs={{0,16},{4,20},{8,24},{12,28},{1,17},{5,21},{9,25},{13,29},{2,18},{... | collective-permute-start | bytes 884744 | tf_op jit(solution)/shard_map/ppermute | solution.py:12
  167.9 18.1 %collective-permute-start.11 = (bf16[128,1152]{0,1:T(8,128)(2,1)S(1)}, bf16[128,1152]{0,1:T(8,128)(2,1)S(1)}, u32[]{:S(2)}, u32[]{:S(2)}) collective-permute-start(bf16[128,1152]{0,1:T(8,128)(2,1)S(1)} %convolution_convert_fusion.3), channel_id=1, source_target_pairs={{16,0},{20,4},{24,8},{28,12},{17,1},{21,5},{25,9},{29,13},{18,2},{... | collective-permute-start | bytes 884744 | tf_op jit(solution)/shard_map/ppermute | solution.py:12
where the time goes:
time: 188 us
  blocking collectives  81.5 us (43%)
  waiting for transfers between devices  37.5 us (20%)
  starting transfers between devices  35.3 us (19%)
  local copies, waits for them, and re-layouts  16.1 us (9%)
  matrix products  15.8 us (8%)
    ppermute x12, waiting for transfers between devices, from_behind(): return lax.ppermute(shard, axis, pairs)  37.5 us
    ppermute x12, starting transfers between devices, from_behind(): return lax.ppermute(shard, axis, pairs)  35.3 us
    all_gather x3, blocking collectives, on_device(): lax.all_gather(diag_rows, 'panel', axis=0, tiled=True)  22 us
    all_gather x3, blocking collectives, on_device(): lax.all_gather(upper_rows, 'panel', axis=0, tiled=True)  21.6 us
    all_gather x3, blocking collectives, on_device(): lax.all_gather(lower_rows, 'panel', axis=0, tiled=True)  20.7 us
    all_gather x3, blocking collectives, on_device(): lax.all_gather(rhs_rows, 'panel', axis=0, tiled=True)  17.2 us
    gather x3, local copies, waits for them, and re-layouts, start_inverse(): inverse_diag = 1.0 / jnp.diagonal(diag_block).astype(jnp.float32)  14.3 us
    dot_general x3, matrix products, on_device(): jnp.dot(inverse, stacked, preferred_element_type=jnp.float32)  7.93 us
  transfers between devices with their start and end apart: 12, of which 5 were waited for; matrix products, arithmetic and copies ran while one was open for 16% of the time, Pallas kernels for 0%

commit v1 on v0

v1 whole, which is shorter than its diff:
```python
import functools

import jax
import jax.numpy as jnp
from jax import lax
from jax.experimental import pallas as pl
from jax.experimental.pallas import tpu as pltpu
from jax.sharding import PartitionSpec as P

LEVELS = 3
LANES = 128
F32 = jnp.float32
BF16 = jnp.bfloat16


def dot_nn(a, b):
    return jnp.dot(a, b, preferred_element_type=F32)


def dot_nt(a, b):
    return lax.dot_general(a, b, (((1,), (1,)), ((), ())), preferred_element_type=F32)


def first_guess(diag_block):
    order = diag_block.shape[0]
    rows = lax.broadcasted_iota(jnp.int32, (order, order), 0)
    cols = lax.broadcasted_iota(jnp.int32, (order, order), 1)
    block = diag_block.astype(F32)
    eye = rows == cols
    only_diag = jnp.where(eye, block, 0.0)
    s_row = 1.0 / jnp.sum(only_diag, axis=0, keepdims=True)
    s_col = 1.0 / jnp.sum(only_diag, axis=1, keepdims=True)
    return (jnp.where(eye, 2.0 * s_row, 0.0) - s_col * block * s_row).astype(BF16)


def kernel(
    layers, panels, l_in, b_in, u_in, f_in, b_out, f_out,
    b_full, l_full, u_full, f_own, p_own, p_near, f_turn, b_turn, b_land, f_land,
    send_sems, recv_sems,
):
    blk, order = l_in.shape
    rhs = f_in.shape[1]
    fb = rhs // panels
    width = 2 * blk + fb
    layer = lax.axis_index("layer")
    panel = lax.axis_index("panel")
    parity = layer % 2
    counter = [0]
    sends = []

    def when(cond, action):
        if cond is None:
            action()
        else:
            pl.when(cond)(action)

    def exists(index):
        return jnp.logical_and(index >= 0, index < layers)

    def flip(index, offset):
        bit = 1
        while bit < panels:
            if offset & bit:
                index = index + bit - 2 * bit * ((index // bit) % 2)
            bit *= 2
        return index

    def copy(src, dst, where):
        n = counter[0]
        counter[0] += 1
        return pltpu.make_async_remote_copy(
            src_ref=src, dst_ref=dst, send_sem=send_sems.at[n], recv_sem=recv_sems.at[n],
            device_id=where, device_id_type=pl.DeviceIdType.MESH,
        )

    def launch(item, cond=None):
        when(cond, item.start)
        sends.append((item, cond))

    def own_rows(index):
        return pl.ds(pl.multiple_of(index * blk, blk), blk)

    mine = own_rows(panel)
    bits = []
    bit = panels // 2
    while bit >= 1:
        bits.append(bit)
        bit //= 2

    def gather_begin(source, full):
        plan, delivered, have = [], {}, [0]
        for bit in bits:
            for off in have:
                rows = own_rows(flip(panel, off))
                src = source if off == 0 else full.at[rows]
                item = copy(src, full.at[rows], {"panel": flip(panel, bit)})
                plan.append((off, item))
                delivered[bit ^ off] = item
            have = have + [o ^ bit for o in have]
        for off, item in plan:
            if off == 0:
                launch(item)
        return plan, delivered, set()

    def gather_forward(state):
        plan, delivered, done = state
        for off, item in plan:
            if off != 0:
                if off not in done:
                    delivered[off].wait_recv()
                    done.add(off)
                launch(item)

    def gather_end(state):
        plan, delivered, done = state
        for off in sorted(delivered):
            if off not in done:
                delivered[off].wait_recv()
                done.add(off)

    barrier = pltpu.get_barrier_semaphore()
    met = jnp.int32(0)
    for off in range(1, panels):
        pl.semaphore_signal(barrier, inc=1, device_id={"panel": (panel + off) % panels})
        met = met + 1
    partner = layer + 1 - 2 * parity
    others = [partner]
    for k in range(1, LEVELS):
        others += [layer - 2**k, layer + 2**k]
    for other in others:
        there = exists(other)

        def greet(other=other):
            pl.semaphore_signal(barrier, inc=1, device_id={"layer": other})

        pl.when(there)(greet)
        met = met + there.astype(jnp.int32)
    pl.semaphore_wait(barrier, met)

    state_b = gather_begin(b_in, b_full.at[0])
    f_turn[...] = f_in[...].T
    state_l = gather_begin(l_in, l_full.at[0])
    state_u = gather_begin(u_in, u_full.at[0])

    def f_rows(index):
        return pl.ds(pl.multiple_of(index * fb, fb), fb)

    f_items = []
    for off in range(1, panels):
        to = (panel + off) % panels
        item = copy(f_turn.at[f_rows(to)], f_own.at[0, :, mine], {"panel": to})
        launch(item)
        f_items.append(item)
    f_own[0, :, mine] = f_turn[f_rows(panel), :]
    b_full[0, mine, :] = b_in[...]
    l_full[0, mine, :] = l_in[...]
    u_full[0, mine, :] = u_in[...]

    for k in range(LEVELS):
        for slot, near in ((0, layer - 2**k), (1, layer + 2**k)):

            def clear(k=k, slot=slot):
                p_near[k, slot] = jnp.zeros((width, order), BF16)

            pl.when(jnp.logical_not(exists(near)))(clear)

    part_a = slice(0, blk)
    part_u = slice(blk + fb, width)
    part_af = slice(0, blk + fb)
    part_fu = slice(blk, width)

    for k in range(LEVELS):
        reach = 2**k
        last = k == LEVELS - 1
        gather_forward(state_b)
        gather_end(state_b)
        bt = b_full[k]
        guess = first_guess(bt)
        if k == 0:
            half = dot_nn(guess, bt).astype(BF16)
            gather_forward(state_l)
            inverse = (2.0 * guess.astype(F32) - dot_nn(half, guess)).astype(BF16)
            gather_forward(state_u)
            gather_end(state_l)
            gather_end(state_u)
            for item in f_items:
                item.wait_recv()
            own_l = l_full[0, :, mine].T
            own_u = u_full[0, :, mine].T
            own_b = b_full[0, :, mine].T
        else:
            half = dot_nn(bt, guess).astype(BF16)
            inverse = (2.0 * guess.astype(F32) - dot_nn(guess, half)).astype(BF16)
            own_l = l_full[k, mine, :]
            own_u = u_full[k, mine, :]
            own_b = b_full[k, mine, :]
        own_f = f_own[k]
        dot = dot_nt if k == 0 else dot_nn
        stacked = jnp.concatenate([own_l, own_f, own_u], axis=0)
        p_own[k] = dot(stacked, inverse).astype(BF16)

        arrivals = {0: [], 1: []}
        if k == 0:
            relays = []
            for part in (part_af, part_u):
                rows = pl.ds(part.start, part.stop - part.start)
                item = copy(
                    p_own.at[0, rows], p_near.at[0, parity, rows], {"layer": partner}
                )
                launch(item)
                relays.append((rows, item))
            onward = layer + 2 - 4 * parity
            origin = layer - 2 + 4 * parity
            late = []
            for rows, item in relays:
                item.wait_recv()
                again = copy(
                    p_near.at[0, 1 - parity, rows], p_near.at[0, parity, rows],
                    {"layer": onward},
                )
                launch(again, exists(onward))
                late.append(again)
            for again in late:
                pl.when(exists(origin))(again.wait_recv)
        else:
            parts = {0: (part_af, part_u), 1: (part_af, part_u)}
            if last:
                parts = {0: (part_fu,), 1: (part_af,)}
            for index in range(max(len(parts[0]), len(parts[1]))):
                for slot, to, origin in (
                    (0, layer + reach, layer - reach),
                    (1, layer - reach, layer + reach),
                ):
                    part = parts[slot][index]
                    rows = pl.ds(part.start, part.stop - part.start)
                    item = copy(p_own.at[k, rows], p_near.at[k, slot, rows], {"layer": to})
                    launch(item, exists(to))
                    arrivals[slot].append((item, exists(origin)))
            gather_forward(state_l)
            gather_forward(state_u)
            gather_end(state_l)
            gather_end(state_u)
            for slot in (0, 1):
                for item, cond in arrivals[slot]:
                    pl.when(cond)(item.wait_recv)

        left = dot(p_near[k, 0, part_fu, :], l_full[k])
        right = dot(p_near[k, 1, part_af, :], u_full[k])
        new_b = (own_b.astype(F32) - left[fb:] - right[:blk]).astype(BF16)
        new_f = (own_f.astype(F32) - left[:fb] - right[blk:]).astype(BF16)
        if not last:
            b_full[k + 1, mine, :] = new_b
            f_own[k + 1] = new_f
            new_l = -dot(p_near[k, 0, part_a, :], l_full[k])
            l_full[k + 1, mine, :] = new_l.astype(BF16)
            state_b = gather_begin(b_full.at[k + 1, mine], b_full.at[k + 1])
            new_u = -dot(p_near[k, 1, part_u, :], u_full[k])
            u_full[k + 1, mine, :] = new_u.astype(BF16)
            state_l = gather_begin(l_full.at[k + 1, mine], l_full.at[k + 1])
            state_u = gather_begin(u_full.at[k + 1, mine], u_full.at[k + 1])
        else:
            f_own[k + 1] = new_f
            b_turn[...] = new_b.T

    landings = []
    for off in range(1, panels):
        to = (panel + off) % panels
        item = copy(b_turn.at[own_rows(to)], b_land.at[:, mine], {"panel": to})
        launch(item)
        landings.append(item)
        item = copy(
            f_own.at[LEVELS, :, own_rows(to)], f_land.at[f_rows(panel)], {"panel": to}
        )
        launch(item)
        landings.append(item)
    b_land[:, mine] = b_turn[mine, :]
    f_land[f_rows(panel), :] = f_own[LEVELS, :, mine]
    for item in landings:
        item.wait_recv()
    b_out[...] = b_land[...]
    f_out[...] = f_land[...].T
    for item, cond in sends:
        when(cond, item.wait_send)


def on_device_kernel(layers, panels, lower_blocks, diag_blocks, upper_blocks, right_sides):
    _, blk, order = lower_blocks.shape
    rhs = right_sides.shape[2]
    fb = rhs // panels
    width = 2 * blk + fb
    copies = 160
    vmem = pl.BlockSpec(memory_space=pltpu.VMEM)
    new_diag, new_rhs = pl.pallas_call(
        functools.partial(kernel, layers, panels),
        out_shape=(
            jax.ShapeDtypeStruct((blk, order), BF16),
            jax.ShapeDtypeStruct((blk, rhs), BF16),
        ),
        in_specs=[vmem] * 4,
        out_specs=(vmem, vmem),
        scratch_shapes=[
            pltpu.VMEM((LEVELS, order, order), BF16),
            pltpu.VMEM((LEVELS, order, order), BF16),
            pltpu.VMEM((LEVELS, order, order), BF16),
            pltpu.VMEM((LEVELS + 1, fb, order), BF16),
            pltpu.VMEM((LEVELS, width, order), BF16),
            pltpu.VMEM((LEVELS, 2, width, order), BF16),
            pltpu.VMEM((rhs, blk), BF16),
            pltpu.VMEM((order, blk), BF16),
            pltpu.VMEM((blk, order), BF16),
            pltpu.VMEM((rhs, blk), BF16),
            pltpu.SemaphoreType.DMA((copies,)),
            pltpu.SemaphoreType.DMA((copies,)),
        ],
        compiler_params=pltpu.CompilerParams(collective_id=0, has_side_effects=True),
    )(lower_blocks[0], diag_blocks[0], upper_blocks[0], right_sides[0])
    return new_diag[None], new_rhs[None]


def from_behind(shard, axis, by):
    size = lax.axis_size(axis)
    pairs = [(i, i + by) for i in range(size) if 0 <= i + by < size]
    return lax.ppermute(shard, axis, pairs)


def start_inverse(diag_block):
    inverse_diag = 1.0 / jnp.diagonal(diag_block).astype(F32)
    identity = jnp.eye(diag_block.shape[0], dtype=F32)
    guess = (
        2.0 * identity * inverse_diag[:, None]
        - inverse_diag[:, None] * diag_block.astype(F32) * inverse_diag[None, :]
    )
    return guess.astype(BF16)


def eliminate(diag_rows, rhs_rows, terms_left, terms_right, order):
    new_lower = (-terms_left[..., :order]).astype(BF16)
    new_diag = (
        diag_rows.astype(F32) - terms_left[..., order : 2 * order] - terms_right[..., :order]
    ).astype(BF16)
    new_upper = (-terms_right[..., order : 2 * order]).astype(BF16)
    new_rhs = (
        rhs_rows.astype(F32) - terms_left[..., 2 * order :] - terms_right[..., 2 * order :]
    ).astype(BF16)
    return new_lower, new_diag, new_upper, new_rhs


def on_device_narrow(lower_blocks, diag_blocks, upper_blocks, right_sides):
    lower_rows, diag_rows = lower_blocks[0], diag_blocks[0]
    upper_rows, rhs_rows = upper_blocks[0], right_sides[0]
    order = lower_rows.shape[1]
    for level_index in range(LEVELS):
        reach = 2**level_index
        full_diag, full_lower, full_upper, full_rhs = (
            lax.all_gather(rows, "panel", axis=0, tiled=True)
            for rows in (diag_rows, lower_rows, upper_rows, rhs_rows)
        )
        stacked = jnp.concatenate([full_lower, full_upper, full_rhs], axis=1)
        guess = start_inverse(full_diag)
        product = dot_nn(guess, full_diag).astype(BF16)
        inverse = (2.0 * guess.astype(F32) - dot_nn(product, guess)).astype(BF16)
        solved = dot_nn(inverse, stacked).astype(BF16)
        coupling_next = from_behind(lower_rows, "layer", -reach)
        coupling_prev = from_behind(upper_rows, "layer", reach)
        partial_next = dot_nn(coupling_next, solved).astype(BF16)
        partial_prev = dot_nn(coupling_prev, solved).astype(BF16)
        terms_left = from_behind(partial_next, "layer", reach).astype(F32)
        terms_right = from_behind(partial_prev, "layer", -reach).astype(F32)
        lower_rows, diag_rows, upper_rows, rhs_rows = eliminate(
            diag_rows, rhs_rows, terms_left, terms_right, order
        )
    return diag_rows[None], rhs_rows[None]


def solution(mesh):
    layers, panels = mesh.shape["layer"], mesh.shape["panel"]
    spec = P("layer", "panel", None)

    def on_device(lower_blocks, diag_blocks, upper_blocks, right_sides):
        blk = lower_blocks.shape[1]
        fb = right_sides.shape[2] // panels
        aligned = blk % LANES == 0 and fb % 16 == 0 and panels & (panels - 1) == 0
        if aligned and layers % 2 == 0:
            return on_device_kernel(
                layers, panels, lower_blocks, diag_blocks, upper_blocks, right_sides
            )
        return on_device_narrow(lower_blocks, diag_blocks, upper_blocks, right_sides)

    return jax.shard_map(
        on_device, mesh=mesh, in_specs=(spec,) * 4, out_specs=(spec, spec), check_vma=False
    )
```

time: 188 us -> 73.6 us (0.39)
  blocking collectives: 81.5 us -> 0 us
  Pallas kernels: 0 us -> 70.6 us
  waiting for transfers between devices: 37.5 us -> 0 us
  starting transfers between devices: 35.3 us -> 0 us
  matrix products: 15.8 us -> 0 us
  local copies, waits for them, and re-layouts: 16.1 us -> 2.19 us
    all_gather x12 -> x0, blocking collectives: 81.5 us -> none  [the longest x3 22 us: on_device(): lax.all_gather(diag_rows, 'panel', axis=0, tiled=True)]
    pallas_call x0 -> x1, Pallas kernels: none -> 70.6 us  [on_device_kernel(): pl.pallas_call(functools.partial(kernel, layers, panels), out_shape=(jax....]
    ppermute x12 -> x0, waiting for transfers between devices: 37.5 us -> none  [from_behind(): return lax.ppermute(shard, axis, pairs)]
    ppermute x12 -> x0, starting transfers between devices: 35.3 us -> none  [from_behind(): return lax.ppermute(shard, axis, pairs)]
    dot_general x12 -> x0, matrix products: 15.8 us -> none  [the longest x3 7.93 us: on_device(): jnp.dot(inverse, stacked, preferred_element_type=jnp.float32)]
    gather x3 -> x0, local copies, waits for them, and re-layouts: 14.3 us -> none  [start_inverse(): inverse_diag = 1.0 / jnp.diagonal(diag_block).astype(jnp.float32)]
  transfers between devices with their start and end apart: 12 -> 0, of which waited for: 5 -> 0; matrix products, arithmetic and copies ran while one was open for 16% -> 0% of each run, Pallas kernels for 0% -> 0%
where the time goes in v1:
time: 73.6 us; the launch traced here: 73.4 us
  Pallas kernels  70.6 us (96%)
  local copies, waits for them, and re-layouts  2.19 us (3%)
    pallas_call x1, Pallas kernels, on_device_kernel(): pl.pallas_call(functools.partial(kernel, layers, panels), out_shape=(jax....  70.6 us
    unnamed x4, local copies, waits for them, and re-layouts  2.19 us

profile of v1, /device:TPU:0, one launch (start us, length us, event | category | flops | bytes accessed | tf_op | source)
XLA Modules:
  0.0 73.4 jit_solution(7851667271295036561)
XLA Ops:
  0.6 70.6 %shard_map.59 = (bf16[128,512]{1,0:T(8,128)(2,1)}, bf16[128,128]{1,0:T(8,128)(2,1)}) custom-call(bf16[128,512]{1,0:T(8,128)(2,1)} %bitcast.6, bf16[128,512]{1,0:T(8,128)(2,1)} %bitcast.7, bf16[128,512]{1,0:T(8,128)(2,1)} %bitcast.8, bf16[128,128]{1,0:T(8,128)(2,1)} %bitcast.11), custom_call_target="tpu_custom_call" | custom-call | tf_op jit(solution)/shard_map/pallas_call | solution.py:293
  71.2 0.0 copy-start
  71.2 1.6 %copy.8 = bf16[1,128,512]{2,1,0:T(8,128)(2,1)} copy(bf16[1,128,512]{2,1,0:T(8,128)(2,1)} %bitcast.9) | data formatting | bytes 262144
  72.8 0.0 copy-done
  72.8 0.6 copy.9
Async XLA Ops:
  71.2 1.6 %copy-start = (bf16[128,128]{1,0:T(8,128)(2,1)S(1)}, bf16[128,128]{1,0:T(8,128)(2,1)}, u32[]{:S(2)}) copy-start(bf16[128,128]{1,0:T(8,128)(2,1)} %get-tuple-element.5) | copy-start | bytes 98308

commit v2 on v1

--- a/solution.py
+++ b/solution.py
@@ -35,7 +35,7 @@
 
 def kernel(
     layers, panels, l_in, b_in, u_in, f_in, b_out, f_out,
-    b_full, l_full, u_full, f_own, p_own, p_near, f_turn, b_turn, b_land, f_land,
+    b_full, l_full, u_full, l_cols, u_cols, f_own, p_own, p_near, f_turn, b_turn, b_land, f_land,
     send_sems, recv_sems,
 ):
     blk, order = l_in.shape
@@ -87,7 +87,7 @@
         bits.append(bit)
         bit //= 2
 
-    def gather_begin(source, full):
+    def gather_begin(source, full, cond=None):
         plan, delivered, have = [], {}, [0]
         for bit in bits:
             for off in have:
@@ -99,23 +99,23 @@
             have = have + [o ^ bit for o in have]
         for off, item in plan:
             if off == 0:
-                launch(item)
-        return plan, delivered, set()
+                launch(item, cond)
+        return plan, delivered, set(), cond
 
     def gather_forward(state):
-        plan, delivered, done = state
+        plan, delivered, done, cond = state
         for off, item in plan:
             if off != 0:
                 if off not in done:
-                    delivered[off].wait_recv()
+                    when(cond, delivered[off].wait_recv)
                     done.add(off)
-                launch(item)
+                launch(item, cond)
 
     def gather_end(state):
-        plan, delivered, done = state
+        plan, delivered, done, cond = state
         for off in sorted(delivered):
             if off not in done:
-                delivered[off].wait_recv()
+                when(cond, delivered[off].wait_recv)
                 done.add(off)
 
     barrier = pltpu.get_barrier_semaphore()
@@ -139,28 +139,38 @@
 
     state_b = gather_begin(b_in, b_full.at[0])
     f_turn[...] = f_in[...].T
+    col_items = []
+    for source, target in ((l_in, l_cols), (u_in, u_cols)):
+        for off in range(1, panels):
+            to = flip(panel, panels - off)
+            item = copy(source.at[:, own_rows(to)], target.at[mine], {"panel": to})
+            launch(item)
+            col_items.append(item)
+
+    def f_rows(index):
+        return pl.ds(pl.multiple_of(index * fb, fb), fb)
+
+    for off in range(1, panels):
+        to = flip(panel, panels - off)
+        item = copy(f_turn.at[f_rows(to)], f_own.at[0, :, mine], {"panel": to})
+        launch(item)
+        col_items.append(item)
     state_l = gather_begin(l_in, l_full.at[0])
     state_u = gather_begin(u_in, u_full.at[0])
-
-    def f_rows(index):
-        return pl.ds(pl.multiple_of(index * fb, fb), fb)
-
-    f_items = []
-    for off in range(1, panels):
-        to = (panel + off) % panels
-        item = copy(f_turn.at[f_rows(to)], f_own.at[0, :, mine], {"panel": to})
-        launch(item)
-        f_items.append(item)
     f_own[0, :, mine] = f_turn[f_rows(panel), :]
     b_full[0, mine, :] = b_in[...]
     l_full[0, mine, :] = l_in[...]
     u_full[0, mine, :] = u_in[...]
+    l_cols[mine, :] = l_in[:, mine]
+    u_cols[mine, :] = u_in[:, mine]
 
     for k in range(LEVELS):
-        for slot, near in ((0, layer - 2**k), (1, layer + 2**k)):
-
-            def clear(k=k, slot=slot):
+        for slot, near, full in ((0, layer - 2**k, l_full), (1, layer + 2**k, u_full)):
+
+            def clear(k=k, slot=slot, full=full):
                 p_near[k, slot] = jnp.zeros((width, order), BF16)
+                if k == LEVELS - 1:
+                    full[k] = jnp.zeros((order, order), BF16)
 
             pl.when(jnp.logical_not(exists(near)))(clear)
 
@@ -168,6 +178,10 @@
     part_u = slice(blk + fb, width)
     part_af = slice(0, blk + fb)
     part_fu = slice(blk, width)
+
+    def wait_all(items):
+        for item, cond in items:
+            when(cond, item.wait_recv)
 
     for k in range(LEVELS):
         reach = 2**k
@@ -178,15 +192,11 @@
         guess = first_guess(bt)
         if k == 0:
             half = dot_nn(guess, bt).astype(BF16)
-            gather_forward(state_l)
             inverse = (2.0 * guess.astype(F32) - dot_nn(half, guess)).astype(BF16)
-            gather_forward(state_u)
-            gather_end(state_l)
-            gather_end(state_u)
-            for item in f_items:
+            for item in col_items:
                 item.wait_recv()
-            own_l = l_full[0, :, mine].T
-            own_u = u_full[0, :, mine].T
+            own_l = l_cols[...].T
+            own_u = u_cols[...].T
             own_b = b_full[0, :, mine].T
         else:
             half = dot_nn(bt, guess).astype(BF16)
@@ -199,68 +209,89 @@
         stacked = jnp.concatenate([own_l, own_f, own_u], axis=0)
         p_own[k] = dot(stacked, inverse).astype(BF16)
 
-        arrivals = {0: [], 1: []}
+        first, second = [], []
         if k == 0:
-            relays = []
-            for part in (part_af, part_u):
-                rows = pl.ds(part.start, part.stop - part.start)
-                item = copy(
-                    p_own.at[0, rows], p_near.at[0, parity, rows], {"layer": partner}
-                )
-                launch(item)
-                relays.append((rows, item))
             onward = layer + 2 - 4 * parity
             origin = layer - 2 + 4 * parity
-            late = []
-            for rows, item in relays:
-                item.wait_recv()
+            piece = blk // 2
+            plan = []
+            for base in (parity * (blk + fb), (1 - parity) * (blk + fb)):
+                for start in (0, piece):
+                    plan.append(pl.ds(pl.multiple_of(base + start, 16), piece))
+            plan.append(pl.ds(blk, fb))
+            direct = []
+            for rows in plan:
+                item = copy(p_own.at[0, rows], p_near.at[0, parity, rows], {"layer": partner})
+                launch(item)
+                direct.append(item)
+            relays = []
+            for index, rows in enumerate(plan):
+                if index < 4:
+                    base = (1 - parity if index < 2 else parity) * (blk + fb)
+                    rows = pl.ds(pl.multiple_of(base + (index % 2) * piece, 16), piece)
                 again = copy(
                     p_near.at[0, 1 - parity, rows], p_near.at[0, parity, rows],
                     {"layer": onward},
                 )
-                launch(again, exists(onward))
-                late.append(again)
-            for again in late:
-                pl.when(exists(origin))(again.wait_recv)
+                relays.append(again)
+            for index in (0, 1):
+                direct[index].wait_recv()
+                launch(relays[index], exists(onward))
+            gather_forward(state_l)
+            for index in (2, 3):
+                direct[index].wait_recv()
+                launch(relays[index], exists(onward))
+            gather_forward(state_u)
+            direct[4].wait_recv()
+            launch(relays[4], exists(onward))
+            first = [(relays[index], exists(origin)) for index in (0, 1)]
+            second = [(relays[index], exists(origin)) for index in (2, 3, 4)]
         else:
-            parts = {0: (part_af, part_u), 1: (part_af, part_u)}
+            stages = (((0, part_u), (1, part_a)), ((0, part_af), (1, part_fu)))
             if last:
-                parts = {0: (part_fu,), 1: (part_af,)}
-            for index in range(max(len(parts[0]), len(parts[1]))):
-                for slot, to, origin in (
-                    (0, layer + reach, layer - reach),
-                    (1, layer - reach, layer + reach),
-                ):
-                    part = parts[slot][index]
+                stages = (((0, part_fu), (1, part_af)),)
+            for stage, group in zip(stages, (first, second)):
+                for slot, part in stage:
+                    to = layer + reach if slot == 0 else layer - reach
+                    origin = layer - reach if slot == 0 else layer + reach
                     rows = pl.ds(part.start, part.stop - part.start)
                     item = copy(p_own.at[k, rows], p_near.at[k, slot, rows], {"layer": to})
                     launch(item, exists(to))
-                    arrivals[slot].append((item, exists(origin)))
+                    group.append((item, exists(origin)))
             gather_forward(state_l)
             gather_forward(state_u)
-            gather_end(state_l)
-            gather_end(state_u)
-            for slot in (0, 1):
-                for item, cond in arrivals[slot]:
-                    pl.when(cond)(item.wait_recv)
-
-        left = dot(p_near[k, 0, part_fu, :], l_full[k])
-        right = dot(p_near[k, 1, part_af, :], u_full[k])
-        new_b = (own_b.astype(F32) - left[fb:] - right[:blk]).astype(BF16)
-        new_f = (own_f.astype(F32) - left[:fb] - right[blk:]).astype(BF16)
-        if not last:
+        gather_end(state_l)
+        gather_end(state_u)
+        wait_all(first)
+        if last:
+            left = dot(p_near[k, 0, part_fu, :], l_full[k])
+            right = dot(p_near[k, 1, part_af, :], u_full[k])
+            new_b = (own_b.astype(F32) - left[fb:] - right[:blk]).astype(BF16)
+            b_turn[...] = new_b.T
+            new_f = (own_f.astype(F32) - left[:fb] - right[blk:]).astype(BF16)
+            f_own[k + 1] = new_f
+        else:
+            left = dot(p_near[k, 0, part_u, :], l_full[k])
+            right = dot(p_near[k, 1, part_a, :], u_full[k])
+            new_b = (own_b.astype(F32) - left - right).astype(BF16)
             b_full[k + 1, mine, :] = new_b
-            f_own[k + 1] = new_f
-            new_l = -dot(p_near[k, 0, part_a, :], l_full[k])
-            l_full[k + 1, mine, :] = new_l.astype(BF16)
             state_b = gather_begin(b_full.at[k + 1, mine], b_full.at[k + 1])
-            new_u = -dot(p_near[k, 1, part_u, :], u_full[k])
-            u_full[k + 1, mine, :] = new_u.astype(BF16)
-            state_l = gather_begin(l_full.at[k + 1, mine], l_full.at[k + 1])
-            state_u = gather_begin(u_full.at[k + 1, mine], u_full.at[k + 1])
-        else:
-            f_own[k + 1] = new_f
-            b_turn[...] = new_b.T
+            wait_all(second)
+            before_last = k + 1 == LEVELS - 1
+            ahead = 2 ** (k + 1)
+            left = dot(p_near[k, 0, part_af, :], l_full[k])
+            l_full[k + 1, mine, :] = (-left[:blk]).astype(BF16)
+            state_l = gather_begin(
+                l_full.at[k + 1, mine], l_full.at[k + 1],
+                exists(layer - ahead) if before_last else None,
+            )
+            right = dot(p_near[k, 1, part_fu, :], u_full[k])
+            u_full[k + 1, mine, :] = (-right[fb:]).astype(BF16)
+            state_u = gather_begin(
+                u_full.at[k + 1, mine], u_full.at[k + 1],
+                exists(layer + ahead) if before_last else None,
+            )
+            f_own[k + 1] = (own_f.astype(F32) - left[blk:] - right[:fb]).astype(BF16)
 
     landings = []
     for off in range(1, panels):
@@ -302,6 +333,8 @@
             pltpu.VMEM((LEVELS, order, order), BF16),
             pltpu.VMEM((LEVELS, order, order), BF16),
             pltpu.VMEM((LEVELS, order, order), BF16),
+            pltpu.VMEM((order, blk), BF16),
+            pltpu.VMEM((order, blk), BF16),
             pltpu.VMEM((LEVELS + 1, fb, order), BF16),
             pltpu.VMEM((LEVELS, width, order), BF16),
             pltpu.VMEM((LEVELS, 2, width, order), BF16),

time: 73.6 us -> 63.2 us (0.86)
  Pallas kernels: 70.6 us -> 60.2 us
    pallas_call x1, Pallas kernels: 70.6 us -> 60.2 us  [on_device_kernel(): pl.pallas_call(functools.partial(kernel, layers, panels), out_shape=(jax....]
where the time goes in v2:
time: 63.2 us; the launch traced here: 63 us
  Pallas kernels  60.2 us (95%)
  local copies, waits for them, and re-layouts  2.19 us (3%)
  between operations  0.65 us (1%)
    pallas_call x1, Pallas kernels, on_device_kernel(): pl.pallas_call(functools.partial(kernel, layers, panels), out_shape=(jax....  60.2 us
    unnamed x4, local copies, waits for them, and re-layouts  2.19 us

profile of v2, /device:TPU:0, one launch (start us, length us, event | category | flops | bytes accessed | tf_op | source)
XLA Modules:
  0.0 63.0 jit_solution(9186892540100987957)
XLA Ops:
  0.6 60.2 %shard_map.59 = (bf16[128,512]{1,0:T(8,128)(2,1)}, bf16[128,128]{1,0:T(8,128)(2,1)}) custom-call(bf16[128,512]{1,0:T(8,128)(2,1)} %bitcast.6, bf16[128,512]{1,0:T(8,128)(2,1)} %bitcast.7, bf16[128,512]{1,0:T(8,128)(2,1)} %bitcast.8, bf16[128,128]{1,0:T(8,128)(2,1)} %bitcast.11), custom_call_target="tpu_custom_call" | custom-call | tf_op jit(solution)/shard_map/pallas_call | solution.py:324
  60.8 0.0 copy-start
  60.8 1.6 %copy.8 = bf16[1,128,512]{2,1,0:T(8,128)(2,1)} copy(bf16[1,128,512]{2,1,0:T(8,128)(2,1)} %bitcast.9) | data formatting | bytes 262144
  62.4 0.0 copy-done
  62.4 0.6 copy.9
Async XLA Ops:
  60.8 1.6 %copy-start = (bf16[128,128]{1,0:T(8,128)(2,1)S(1)}, bf16[128,128]{1,0:T(8,128)(2,1)}, u32[]{:S(2)}) copy-start(bf16[128,128]{1,0:T(8,128)(2,1)} %get-tuple-element.5) | copy-start | bytes 98308

commit v3 on v2

--- a/solution.py
+++ b/solution.py
@@ -9,6 +9,7 @@
 
 LEVELS = 3
 LANES = 128
+PIECES = 2
 F32 = jnp.float32
 BF16 = jnp.bfloat16
 
@@ -34,9 +35,9 @@
 
 
 def kernel(
-    layers, panels, l_in, b_in, u_in, f_in, b_out, f_out,
-    b_full, l_full, u_full, l_cols, u_cols, f_own, p_own, p_near, f_turn, b_turn, b_land, f_land,
-    send_sems, recv_sems,
+    layers, panels, l_hbm, b_hbm, u_hbm, f_hbm, b_out, f_out, l_in, b_in, u_in, f_in,
+    b_full, l_full, u_full, l_cols, u_cols, f_own, p_own, p_near, f_turn, b_last, b_land, f_land,
+    send_sems, recv_sems, load_sems,
 ):
     blk, order = l_in.shape
     rhs = f_in.shape[1]
@@ -87,11 +88,14 @@
         bits.append(bit)
         bit //= 2
 
-    def gather_begin(source, full, cond=None):
+    def gather_begin(source, full, cond=None, start=0, size=None):
+        def piece(index):
+            return pl.ds(pl.multiple_of(index * blk + start, 16), size or blk)
+
         plan, delivered, have = [], {}, [0]
         for bit in bits:
             for off in have:
-                rows = own_rows(flip(panel, off))
+                rows = piece(flip(panel, off))
                 src = source if off == 0 else full.at[rows]
                 item = copy(src, full.at[rows], {"panel": flip(panel, bit)})
                 plan.append((off, item))
@@ -102,7 +106,15 @@
                 launch(item, cond)
         return plan, delivered, set(), cond
 
-    def gather_forward(state):
+    def gather_forward(states):
+        for state in states:
+            forward_one(state)
+
+    def gather_end(states):
+        for state in states:
+            end_one(state)
+
+    def forward_one(state):
         plan, delivered, done, cond = state
         for off, item in plan:
             if off != 0:
@@ -111,13 +123,19 @@
                     done.add(off)
                 launch(item, cond)
 
-    def gather_end(state):
+    def end_one(state):
         plan, delivered, done, cond = state
         for off in sorted(delivered):
             if off not in done:
                 when(cond, delivered[off].wait_recv)
                 done.add(off)
 
+    loads = []
+    for n, (src, dst) in enumerate(
+        ((b_hbm, b_in), (l_hbm, l_in), (u_hbm, u_in), (f_hbm, f_in))
+    ):
+        loads.append(pltpu.make_async_copy(src, dst, load_sems.at[n]))
+        loads[n].start()
     barrier = pltpu.get_barrier_semaphore()
     met = jnp.int32(0)
     for off in range(1, panels):
@@ -135,9 +153,19 @@
 
         pl.when(there)(greet)
         met = met + there.astype(jnp.int32)
+    for item in loads:
+        item.wait()
     pl.semaphore_wait(barrier, met)
 
-    state_b = gather_begin(b_in, b_full.at[0])
+    half_rows = blk // PIECES
+    state_b = []
+    for h in range(PIECES):
+        state_b.append(
+            gather_begin(
+                b_in.at[pl.ds(h * half_rows, half_rows)], b_full.at[0], None,
+                h * half_rows, half_rows,
+            )
+        )
     f_turn[...] = f_in[...].T
     col_items = []
     for source, target in ((l_in, l_cols), (u_in, u_cols)):
@@ -155,8 +183,8 @@
         item = copy(f_turn.at[f_rows(to)], f_own.at[0, :, mine], {"panel": to})
         launch(item)
         col_items.append(item)
-    state_l = gather_begin(l_in, l_full.at[0])
-    state_u = gather_begin(u_in, u_full.at[0])
+    state_l = [gather_begin(l_in, l_full.at[0])]
+    state_u = [gather_begin(u_in, u_full.at[0])]
     f_own[0, :, mine] = f_turn[f_rows(panel), :]
     b_full[0, mine, :] = b_in[...]
     l_full[0, mine, :] = l_in[...]
@@ -174,19 +202,43 @@
 
             pl.when(jnp.logical_not(exists(near)))(clear)
 
-    part_a = slice(0, blk)
-    part_u = slice(blk + fb, width)
-    part_af = slice(0, blk + fb)
-    part_fu = slice(blk, width)
+    half_a = [slice(h * half_rows, (h + 1) * half_rows) for h in range(PIECES)]
+    half_u = [slice(blk + fb + p.start, blk + fb + p.stop) for p in half_a]
+    part_f = slice(blk, blk + fb)
 
     def wait_all(items):
         for item, cond in items:
             when(cond, item.wait_recv)
 
+    landings = []
+
+    def land_f():
+        for off in range(1, panels):
+            to = flip(panel, panels - off)
+            item = copy(
+                f_own.at[LEVELS, :, own_rows(to)], f_land.at[f_rows(panel)], {"panel": to}
+            )
+            launch(item)
+            landings.append(item)
+        f_land[f_rows(panel), :] = f_own[LEVELS, :, mine]
+
+    def land_b(h):
+        target = pl.ds(pl.multiple_of(panel * blk + h * half_rows, 16), half_rows)
+        for off in range(1, panels):
+            to = flip(panel, panels - off)
+            item = copy(
+                b_last.at[pl.ds(h * half_rows, half_rows), own_rows(to)], b_land.at[target],
+                {"panel": to},
+            )
+            launch(item)
+            landings.append(item)
+        b_land[target, :] = b_last[half_a[h], mine]
+
     for k in range(LEVELS):
         reach = 2**k
         last = k == LEVELS - 1
-        gather_forward(state_b)
+        if k == 0:
+            gather_forward(state_b)
         gather_end(state_b)
         bt = b_full[k]
         guess = first_guess(bt)
@@ -199,119 +251,137 @@
             own_u = u_cols[...].T
             own_b = b_full[0, :, mine].T
         else:
-            half = dot_nn(bt, guess).astype(BF16)
-            inverse = (2.0 * guess.astype(F32) - dot_nn(guess, half)).astype(BF16)
             own_l = l_full[k, mine, :]
             own_u = u_full[k, mine, :]
             own_b = b_full[k, mine, :]
         own_f = f_own[k]
         dot = dot_nt if k == 0 else dot_nn
-        stacked = jnp.concatenate([own_l, own_f, own_u], axis=0)
-        p_own[k] = dot(stacked, inverse).astype(BF16)
-
-        first, second = [], []
+
+        first, second, third = [[] for _ in half_a], [[] for _ in half_a], []
         if k == 0:
+            stacked = jnp.concatenate([own_l, own_f, own_u], axis=0)
+            p_own[0] = dot(stacked, inverse).astype(BF16)
             onward = layer + 2 - 4 * parity
             origin = layer - 2 + 4 * parity
-            piece = blk // 2
-            plan = []
-            for base in (parity * (blk + fb), (1 - parity) * (blk + fb)):
-                for start in (0, piece):
-                    plan.append(pl.ds(pl.multiple_of(base + start, 16), piece))
-            plan.append(pl.ds(blk, fb))
-            direct = []
-            for rows in plan:
+
+            def pieces(side):
+                plan = []
+                for base in (side * (blk + fb), (1 - side) * (blk + fb)):
+                    for part in half_a:
+                        start = pl.multiple_of(base + part.start, 16)
+                        plan.append(pl.ds(start, half_rows))
+                plan.append(pl.ds(blk, fb))
+                return plan
+
+            direct, relays = [], []
+            for rows in pieces(parity):
                 item = copy(p_own.at[0, rows], p_near.at[0, parity, rows], {"layer": partner})
                 launch(item)
                 direct.append(item)
-            relays = []
-            for index, rows in enumerate(plan):
-                if index < 4:
-                    base = (1 - parity if index < 2 else parity) * (blk + fb)
-                    rows = pl.ds(pl.multiple_of(base + (index % 2) * piece, 16), piece)
-                again = copy(
-                    p_near.at[0, 1 - parity, rows], p_near.at[0, parity, rows],
-                    {"layer": onward},
+            for rows in pieces(1 - parity):
+                relays.append(
+                    copy(
+                        p_near.at[0, 1 - parity, rows], p_near.at[0, parity, rows],
+                        {"layer": onward},
+                    )
                 )
-                relays.append(again)
-            for index in (0, 1):
-                direct[index].wait_recv()
-                launch(relays[index], exists(onward))
-            gather_forward(state_l)
-            for index in (2, 3):
-                direct[index].wait_recv()
-                launch(relays[index], exists(onward))
+            for index, (item, again) in enumerate(zip(direct, relays)):
+                if index == PIECES:
+                    gather_forward(state_l)
+                item.wait_recv()
+                launch(again, exists(onward))
             gather_forward(state_u)
-            direct[4].wait_recv()
-            launch(relays[4], exists(onward))
-            first = [(relays[index], exists(origin)) for index in (0, 1)]
-            second = [(relays[index], exists(origin)) for index in (2, 3, 4)]
+            for h in range(PIECES):
+                first[h].append((relays[h], exists(origin)))
+                second[h].append((relays[PIECES + h], exists(origin)))
+            third.append((relays[2 * PIECES], exists(origin)))
         else:
-            stages = (((0, part_u), (1, part_a)), ((0, part_af), (1, part_fu)))
-            if last:
-                stages = (((0, part_fu), (1, part_af)),)
-            for stage, group in zip(stages, (first, second)):
-                for slot, part in stage:
-                    to = layer + reach if slot == 0 else layer - reach
-                    origin = layer - reach if slot == 0 else layer + reach
-                    rows = pl.ds(part.start, part.stop - part.start)
-                    item = copy(p_own.at[k, rows], p_near.at[k, slot, rows], {"layer": to})
-                    launch(item, exists(to))
-                    group.append((item, exists(origin)))
+
+            def exchange(slot, part, group):
+                to = layer + reach if slot == 0 else layer - reach
+                origin = layer - reach if slot == 0 else layer + reach
+                rows = pl.ds(part.start, part.stop - part.start)
+                item = copy(p_own.at[k, rows], p_near.at[k, slot, rows], {"layer": to})
+                launch(item, exists(to))
+                group.append((item, exists(origin)))
+
+            scaled = dot_nn(jnp.concatenate([own_l, own_f, own_u], axis=0), guess)
+            back = dot_nn(scaled.astype(BF16), bt).astype(BF16)
+            p_own[k] = (2.0 * scaled - dot_nn(back, guess)).astype(BF16)
+            for h, (a, u) in enumerate(zip(half_a, half_u)):
+                if h == 0:
+                    if last:
+                        exchange(0, part_f, third)
+                        exchange(1, part_f, third)
+                exchange(0, u, first[h])
+                exchange(1, a, first[h])
+            if not last:
+                for h, (a, u) in enumerate(zip(half_a, half_u)):
+                    exchange(0, a, second[h])
+                    exchange(1, u, second[h])
+                exchange(0, part_f, third)
+                exchange(1, part_f, third)
             gather_forward(state_l)
             gather_forward(state_u)
         gather_end(state_l)
         gather_end(state_u)
-        wait_all(first)
+
+        def new_rhs():
+            wait_all(third)
+            left = dot(p_near[k, 0, part_f, :], l_full[k])
+            right = dot(p_near[k, 1, part_f, :], u_full[k])
+            f_own[k + 1] = (own_f.astype(F32) - left - right).astype(BF16)
+
+        def new_diag(h):
+            wait_all(first[h])
+            left = dot(p_near[k, 0, half_u[h], :], l_full[k])
+            right = dot(p_near[k, 1, half_a[h], :], u_full[k])
+            return (own_b[half_a[h]].astype(F32) - left - right).astype(BF16)
+
+        def share(full, h, value, cond=None):
+            rows = pl.ds(pl.multiple_of(panel * blk + h * half_rows, 16), half_rows)
+            full[k + 1, rows, :] = value
+            return gather_begin(
+                full.at[k + 1, rows], full.at[k + 1], cond, h * half_rows, half_rows
+            )
+
         if last:
-            left = dot(p_near[k, 0, part_fu, :], l_full[k])
-            right = dot(p_near[k, 1, part_af, :], u_full[k])
-            new_b = (own_b.astype(F32) - left[fb:] - right[:blk]).astype(BF16)
-            b_turn[...] = new_b.T
-            new_f = (own_f.astype(F32) - left[:fb] - right[blk:]).astype(BF16)
-            f_own[k + 1] = new_f
+            new_rhs()
+            land_f()
+            for h in range(PIECES):
+                b_last[half_a[h], :] = new_diag(h)
+                land_b(h)
         else:
-            left = dot(p_near[k, 0, part_u, :], l_full[k])
-            right = dot(p_near[k, 1, part_a, :], u_full[k])
-            new_b = (own_b.astype(F32) - left - right).astype(BF16)
-            b_full[k + 1, mine, :] = new_b
-            state_b = gather_begin(b_full.at[k + 1, mine], b_full.at[k + 1])
-            wait_all(second)
+            state_b, state_l, state_u = [], [], []
+            for h in range(PIECES):
+                state_b.append(share(b_full, h, new_diag(h)))
             before_last = k + 1 == LEVELS - 1
             ahead = 2 ** (k + 1)
-            left = dot(p_near[k, 0, part_af, :], l_full[k])
-            l_full[k + 1, mine, :] = (-left[:blk]).astype(BF16)
-            state_l = gather_begin(
-                l_full.at[k + 1, mine], l_full.at[k + 1],
-                exists(layer - ahead) if before_last else None,
-            )
-            right = dot(p_near[k, 1, part_fu, :], u_full[k])
-            u_full[k + 1, mine, :] = (-right[fb:]).astype(BF16)
-            state_u = gather_begin(
-                u_full.at[k + 1, mine], u_full.at[k + 1],
-                exists(layer + ahead) if before_last else None,
-            )
-            f_own[k + 1] = (own_f.astype(F32) - left[blk:] - right[:fb]).astype(BF16)
-
-    landings = []
-    for off in range(1, panels):
-        to = (panel + off) % panels
-        item = copy(b_turn.at[own_rows(to)], b_land.at[:, mine], {"panel": to})
-        launch(item)
-        landings.append(item)
-        item = copy(
-            f_own.at[LEVELS, :, own_rows(to)], f_land.at[f_rows(panel)], {"panel": to}
-        )
-        launch(item)
-        landings.append(item)
-    b_land[:, mine] = b_turn[mine, :]
-    f_land[f_rows(panel), :] = f_own[LEVELS, :, mine]
+            for h in range(PIECES):
+                wait_all(second[h])
+                value = -dot(p_near[k, 0, half_a[h], :], l_full[k])
+                cond = exists(layer - ahead) if before_last else None
+                state_l.append(share(l_full, h, value.astype(BF16), cond))
+                value = -dot(p_near[k, 1, half_u[h], :], u_full[k])
+                cond = exists(layer + ahead) if before_last else None
+                state_u.append(share(u_full, h, value.astype(BF16), cond))
+                if h > 0:
+                    forward_one(state_b[h - 1])
+            forward_one(state_b[PIECES - 1])
+            new_rhs()
+
     for item in landings:
         item.wait_recv()
     b_out[...] = b_land[...]
-    f_out[...] = f_land[...].T
+    f_out[...] = f_land[...]
     for item, cond in sends:
         when(cond, item.wait_send)
+    assert counter[0] == send_sems.shape[0]
+
+
+def hand_over(turned_diag_in, turned_in, diag_out, rhs_out):
+    diag_out[...] = turned_diag_in[...].T
+    rhs_out[...] = turned_in[...].T
 
 
 def on_device_kernel(layers, panels, lower_blocks, diag_blocks, upper_blocks, right_sides):
@@ -319,17 +389,23 @@
     rhs = right_sides.shape[2]
     fb = rhs // panels
     width = 2 * blk + fb
-    copies = 160
+    peers, steps = panels - 1, LEVELS - 1
+    copies = peers * (2 * PIECES + 6 + 3 * PIECES * steps)
+    copies += 2 * (2 * PIECES + 1) * steps + 2 * (PIECES + 1)
     vmem = pl.BlockSpec(memory_space=pltpu.VMEM)
     new_diag, new_rhs = pl.pallas_call(
         functools.partial(kernel, layers, panels),
         out_shape=(
-            jax.ShapeDtypeStruct((blk, order), BF16),
-            jax.ShapeDtypeStruct((blk, rhs), BF16),
+            jax.ShapeDtypeStruct((order, blk), BF16),
+            jax.ShapeDtypeStruct((rhs, blk), BF16),
         ),
-        in_specs=[vmem] * 4,
+        in_specs=[pl.BlockSpec(memory_space=pl.ANY)] * 4,
         out_specs=(vmem, vmem),
         scratch_shapes=[
+            pltpu.VMEM((blk, order), BF16),
+            pltpu.VMEM((blk, order), BF16),
+            pltpu.VMEM((blk, order), BF16),
+            pltpu.VMEM((blk, rhs), BF16),
             pltpu.VMEM((LEVELS, order, order), BF16),
             pltpu.VMEM((LEVELS, order, order), BF16),
             pltpu.VMEM((LEVELS, order, order), BF16),
@@ -339,14 +415,24 @@
             pltpu.VMEM((LEVELS, width, order), BF16),
             pltpu.VMEM((LEVELS, 2, width, order), BF16),
             pltpu.VMEM((rhs, blk), BF16),
+            pltpu.VMEM((blk, order), BF16),
             pltpu.VMEM((order, blk), BF16),
-            pltpu.VMEM((blk, order), BF16),
             pltpu.VMEM((rhs, blk), BF16),
             pltpu.SemaphoreType.DMA((copies,)),
             pltpu.SemaphoreType.DMA((copies,)),
+            pltpu.SemaphoreType.DMA((4,)),
         ],
         compiler_params=pltpu.CompilerParams(collective_id=0, has_side_effects=True),
     )(lower_blocks[0], diag_blocks[0], upper_blocks[0], right_sides[0])
+    new_diag, new_rhs = pl.pallas_call(
+        hand_over,
+        out_shape=(
+            jax.ShapeDtypeStruct((blk, order), BF16),
+            jax.ShapeDtypeStruct((blk, rhs), BF16),
+        ),
+        in_specs=[vmem] * 2,
+        out_specs=(vmem, vmem),
+    )(new_diag, new_rhs)
     return new_diag[None], new_rhs[None]
 
 
@@ -412,7 +498,7 @@
     def on_device(lower_blocks, diag_blocks, upper_blocks, right_sides):
         blk = lower_blocks.shape[1]
         fb = right_sides.shape[2] // panels
-        aligned = blk % LANES == 0 and fb % 16 == 0 and panels & (panels - 1) == 0
+        aligned = blk % LANES == 0 and fb % 16 == 0 and blk // PIECES % 16 == 0 and panels & (panels - 1) == 0
         if aligned and layers % 2 == 0:
             return on_device_kernel(
                 layers, panels, lower_blocks, diag_blocks, upper_blocks, right_sides

time: 63.2 us -> 58.9 us (0.932)
  local copies, waits for them, and re-layouts: 2.19 us -> 0 us
  Pallas kernels: 60.2 us -> 58.2 us
    pallas_call x1, Pallas kernels: 60.2 us -> 56.5 us  [on_device_kernel(): pl.pallas_call(functools.partial(kernel, layers, panels), out_shape=(jax....]
    unnamed x4 -> x0, local copies, waits for them, and re-layouts: 2.19 us -> none
    pallas_call x0 -> x1, Pallas kernels: none -> 1.65 us  [on_device_kernel(): pl.pallas_call(hand_over, out_shape=(jax.ShapeDtypeStruct((blk, order), B...]
where the time goes in v3:
time: 58.9 us; the launch traced here: 58.8 us
  Pallas kernels  58.2 us (99%)
  between operations  0.64 us (1%)
    pallas_call x1, Pallas kernels, on_device_kernel(): pl.pallas_call(functools.partial(kernel, layers, panels), out_shape=(jax....  56.5 us
    pallas_call x1, Pallas kernels, on_device_kernel(): pl.pallas_call(hand_over, out_shape=(jax.ShapeDtypeStruct((blk, order), B...  1.65 us

profile of v3, /device:TPU:0, one launch (start us, length us, event | category | flops | bytes accessed | tf_op | source)
XLA Modules:
  0.0 58.8 jit_solution(16036740495294603242)
XLA Ops:
  0.6 56.5 %shard_map.59 = (bf16[512,128]{1,0:T(8,128)(2,1)}, bf16[128,128]{1,0:T(8,128)(2,1)}) custom-call(bf16[128,512]{1,0:T(8,128)(2,1)} %bitcast.6, bf16[128,512]{1,0:T(8,128)(2,1)} %bitcast.7, bf16[128,512]{1,0:T(8,128)(2,1)} %bitcast.8, bf16[128,128]{1,0:T(8,128)(2,1)} %bitcast.9), custom_call_target="tpu_custom_call" | custom-call | tf_op jit(solution)/shard_map/pallas_call | solution.py:396
  57.1 1.7 %shard_map.60 = (bf16[128,512]{1,0:T(8,128)(2,1)}, bf16[128,128]{1,0:T(8,128)(2,1)}) custom-call(bf16[512,128]{1,0:T(8,128)(2,1)} %get-tuple-element.6.turned_diag_in, bf16[128,128]{1,0:T(8,128)(2,1)} %get-tuple-element.7.turned_in), custom_call_target="tpu_custom_call" | custom-call | tf_op jit(solution)/shard_map/pallas_call | solution.py:427
